TPU v7x, 512 devices: a whole 4x4x16 slice. The times are simulated.
512 devices in a mesh: group: 32 (over x, y, core), tp: 16 (over z).
Axes of the slice: x: 4, y: 4, z: 16, core: 2. Of those that a mesh axis runs over, the one named last changes fastest.
Arguments:
- tokens: bfloat16 [24576, 8192], P('group', 'tp'), may hold values from -6 to 6
- w_query: bfloat16 [8192, 4096], P(None, 'tp'), may hold values from -0.0625 to 0.0625
- adapter_down: bfloat16 [384, 16, 8192], P('group', None, 'tp'), may hold values from -0.0625 to 0.0625
- adapter_up: bfloat16 [384, 16, 4096], P('group', None, 'tp'), may hold values from -1.5 to 1.5
- adapter_id: int32 [24576], P('group'), may hold values from 0 to 383, as said below
Outputs:
- query: bfloat16 [24576, 4096], P('group', 'tp')
Inputs may be any that keep to these rules, and one draw needn't show every extreme that they name: `adapter_id`: adapter a is owned by group a // 12. Among the 768 requests of one group (an aligned block), at most 48 use adapters of any one owner; in every draw one owner receives exactly 48 from every group.
All inputs are finite; a program needn't handle non-finite values.
Results may differ from a plain program's by a relative error of at most 0.014.
Values may be sent and summed in bfloat16 or wider, within the bound.
No kernel may reach another device: no remote copies, remote signals or barrier semaphores. Data moves between devices by JAX's collectives and lax.ppermute only.
A program may use at most 128 MiB of HBM per device.

v0:
```python
import jax
import jax.numpy as jnp
from jax import lax
from jax.sharding import PartitionSpec as P

adapter_scale_factor = 2.0


def on_device(tokens, w_query, adapter_down, adapter_up, adapter_id):
    pool_down, pool_up = (
        lax.all_gather(adapter_down, "group", axis=0, tiled=True),
        lax.all_gather(adapter_up, "group", axis=0, tiled=True),
    )
    picked_down = jnp.take(pool_down, adapter_id, axis=0)
    partial_value = jnp.einsum(
        "nd,nrd->nr", tokens, picked_down, preferred_element_type=jnp.float32
    )
    total_output = lax.psum(partial_value, "tp")
    scaled_delta = (adapter_scale_factor * total_output).astype(jnp.bfloat16)
    picked_up = jnp.take(pool_up, adapter_id, axis=0)
    delta_rows = jnp.einsum(
        "nr,nrh->nh", scaled_delta, picked_up, preferred_element_type=jnp.float32
    ).astype(jnp.bfloat16)
    base = jnp.dot(
        lax.all_gather(tokens, "tp", axis=1, tiled=True),
        w_query,
        preferred_element_type=jnp.float32,
    )
    return (base + delta_rows.astype(jnp.float32)).astype(jnp.bfloat16)


def solution(mesh):
    placed = (
        P("group", "tp"),
        P(None, "tp"),
        P("group", None, "tp"),
        P("group", None, "tp"),
        P("group"),
    )
    return jax.shard_map(
        on_device, mesh=mesh, in_specs=placed, out_specs=P("group", "tp"), check_vma=False
    )
```

profile of v0, /device:TPU:1, one launch (start us, length us, event | category | flops | bytes accessed | tf_op | source)
XLA Modules:
  0.0 317.1 jit_solution(11295828361454792933)
XLA Ops:
  6.5 0.0 all-gather.8.cloned.1.call-start
  6.5 0.7 all-gather.8.cloned.1.call-update
  7.3 0.0 all-gather.6.cloned.1.call-start
  7.3 0.7 all-gather.6.cloned.1.call-update
  8.0 0.0 all-gather.4.cloned.1.call-start
  8.1 0.7 all-gather.4.cloned.1.call-update
  8.7 0.7 compare_select_fusion
  9.4 0.7 compare_and_fusion
  10.1 66.6 %all-gather.8.cloned.1.call-done = bf16[384,16,256]{2,1,0:T(8,128)(2,1)} async-done(((bf16[12,16,256]{2,1,0:T(8,128)(2,1)}), bf16[384,16,256]{2,1,0:T(8,128)(2,1)}) %all-gather.8.cloned.1.call-update) | async-done | bytes 3145744 | tf_op jit(solution)/shard_map/all_gather | solution.py:12
  76.7 7.0 %gather_fusion.1 = bf16[768,16,256]{2,1,0:T(8,128)(2,1)} fusion(bf16[384,16,256]{2,1,0:T(8,128)(2,1)} %all-gather.8.cloned.1.call-done, s32[1024]{0:T(1024)S(1)} %pad_clamp_fusion), kind=kCustom, calls=%fused_computation.1 | custom fusion | bytes 12585984 | tf_op jit(solution)/shard_map/jit(_take)/gather | solution.py:20
  83.6 0.0 copy-start
  83.6 60.0 %all-gather.6.cloned.1.call-done = bf16[384,16,512]{2,1,0:T(8,128)(2,1)} async-done(((bf16[12,16,512]{2,1,0:T(8,128)(2,1)}), bf16[384,16,512]{2,1,0:T(8,128)(2,1)}) %all-gather.6.cloned.1.call-update) | async-done | bytes 6291472 | tf_op jit(solution)/shard_map/all_gather | solution.py:11
  143.7 22.4 %gather_fusion = bf16[768,16,512]{2,1,0:T(8,128)(2,1)} fusion(bf16[384,16,512]{2,1,0:T(8,128)(2,1)} %all-gather.6.cloned.1.call-done, s32[1024]{0:T(1024)S(1)} %pad_clamp_fusion), kind=kCustom, calls=%fused_computation | custom fusion | bytes 25168896 | tf_op jit(solution)/shard_map/jit(_take)/gather | solution.py:14
  166.1 0.0 copy-done
  166.1 9.9 %fusion = f32[768,1,16]{2,1,0:T(1,128)S(1)} fusion(bf16[768,16,512]{2,1,0:T(8,128)(2,1)} %gather_fusion, pred[768]{0:T(1024)(128)(4,1)S(1)} %compare_and_fusion, bf16[768,512,1]{1,0,2:T(8,128)(2,1)S(1)} %bitcast.11), kind=kOutput, calls=%fused_computation.2 | convolution fusion | flops 18874368 | bytes 13419264 | tf_op jit(solution)/shard_map/nd,nrd->nr/dot_general | solution.py:15
  176.1 61.4 %psum.7 = f32[768,16]{1,0:T(8,128)S(1)} all-reduce(f32[768,16]{1,0:T(8,128)S(1)} %bitcast.12), channel_id=1, replica_groups=mesh['group'=32,'tp'=16] {'tp'}, use_global_device_ids=true, to_apply=%region_0.1 | all-reduce | flops 12288 | bytes 98304 | tf_op jit(solution)/shard_map/psum | solution.py:18
  237.5 8.5 %fusion.3 = bf16[768,1,256]{2,1,0:T(2,128)(2,1)S(1)} fusion(bf16[768,16,256]{2,1,0:T(8,128)(2,1)} %gather_fusion.1, pred[768]{0:T(1024)(128)(4,1)S(1)} %compare_and_fusion, bf16[768,16,1]{1,0,2:T(8,128)(2,1)S(1)} %fusion.11), kind=kOutput, calls=%fused_computation.5 | convolution fusion | flops 9437184 | bytes 6710016 | tf_op jit(solution)/shard_map/nr,nrh->nh/dot_general | solution.py:21
  246.0 54.7 %all-gather.4.cloned.1.call-done = bf16[768,8192]{1,0:T(8,128)(2,1)} async-done(((bf16[768,512]{1,0:T(8,128)(2,1)}), bf16[768,8192]{1,0:T(8,128)(2,1)}) %all-gather.4.cloned.1.call-update) | async-done | bytes 12582928 | tf_op jit(solution)/shard_map/all_gather | solution.py:25
  300.7 9.9 %fusion.9 = bf16[768,256]{1,0:T(8,128)(2,1)} fusion(bf16[768,8192]{1,0:T(8,128)(2,1)} %all-gather.4.cloned.1.call-done, bf16[8192,256]{1,0:T(8,128)(2,1)} %param.6, bf16[768,1,256]{2,1,0:T(2,128)(2,1)S(1)} %fusion.3), kind=kOutput, calls=%fused_computation.12 | convolution fusion | flops 3221815296 | bytes 17563648 | tf_op jit(solution)/shard_map/dot_general | solution.py:24
  (2 shorter events, 0.0 us)
Async XLA Ops:
  6.5 70.2 %all-gather.8.cloned.1.call-start = ((), (), s32[]{:S(2)}) async-start(), calls=%async_computation.2 | async-start | bytes 3244032 | tf_op jit(solution)/shard_map/all_gather | solution.py:12
  7.3 136.4 %all-gather.6.cloned.1.call-start = ((), (), s32[]{:S(2)}) async-start(), calls=%async_computation.1 | async-start | bytes 6488064 | tf_op jit(solution)/shard_map/all_gather | solution.py:11
  8.0 292.7 %all-gather.4.cloned.1.call-start = ((), (), s32[]{:S(2)}) async-start(), calls=%async_computation | async-start | bytes 13369344 | tf_op jit(solution)/shard_map/all_gather | solution.py:25
  83.6 82.5 %copy-start = (bf16[768,512]{1,0:T(8,128)(2,1)S(1)}, bf16[768,512]{1,0:T(8,128)(2,1)}, u32[]{:S(2)}) copy-start(bf16[768,512]{1,0:T(8,128)(2,1)} %param.5) | copy-start | bytes 2359300
Sparse Core Ops, SparseCore 0:
  10.5 66.1 all-gather.7
  79.8 63.8 all-gather.5
  145.8 154.8 all-gather.3
where the time goes:
time: 317 us
  waiting for transfers between devices  183 us (58%)
  blocking collectives  61.4 us (19%)
  local copies, waits for them, and re-layouts  29.4 us (9%)
  matrix products  28.3 us (9%)
  between operations  13.2 us (4%)
    all_gather x1, waiting for transfers between devices, on_device(): lax.all_gather(adapter_up, 'group', axis=0, tiled=True)  66.6 us
    psum x1, blocking collectives, on_device(): total_output = lax.psum(partial_value, 'tp')  61.4 us
    all_gather x1, waiting for transfers between devices, on_device(): lax.all_gather(adapter_down, 'group', axis=0, tiled=True)  60 us
    all_gather x1, waiting for transfers between devices, on_device(): lax.all_gather(tokens, 'tp', axis=1, tiled=True)  54.7 us
    gather x1, local copies, waits for them, and re-layouts, on_device(): picked_down = jnp.take(pool_down, adapter_id, axis=0)  22.4 us
    dot_general x1, matrix products, on_device(): jnp.dot(lax.all_gather(tokens, 'tp', axis=1, tiled=True), w_query, prefer...  9.92 us
    dot_general x1, matrix products, on_device(): jnp.einsum('nd,nrd->nr', tokens, picked_down, preferred_element_type=jnp....  9.91 us
    dot_general x1, matrix products, on_device(): jnp.einsum('nr,nrh->nh', scaled_delta, picked_up, preferred_element_type=...  8.51 us
  transfers between devices with their start and end apart: 3, of which 3 were waited for; matrix products, arithmetic and copies ran while one was open for 16% of the time, Pallas kernels for 0%

commit v1 on v0

--- a/solution.py
+++ b/solution.py
@@ -6,9 +6,14 @@
 adapter_scale_factor = 2.0
 
 
+def swapped_in(x, axis, along):
+    repeated = jnp.stack([x] * lax.axis_size(axis))
+    return jnp.concatenate(lax.all_to_all(repeated, axis, 0, 0), axis=along)
+
+
 def on_device(tokens, w_query, adapter_down, adapter_up, adapter_id):
     pool_down, pool_up = (
-        lax.all_gather(adapter_down, "group", axis=0, tiled=True),
+        swapped_in(adapter_down, "group", 0),
         lax.all_gather(adapter_up, "group", axis=0, tiled=True),
     )
     picked_down = jnp.take(pool_down, adapter_id, axis=0)

time: 317 us -> 289 us (0.912)
  waiting for transfers between devices: 183 us -> 137 us
  starting transfers between devices: 0.08 us -> 11.6 us
  local copies, waits for them, and re-layouts: 29.4 us -> 33.9 us
    all_to_all x0 -> x1, waiting for transfers between devices: none -> 80.9 us  [swapped_in(): return jnp.concatenate(lax.all_to_all(repeated, axis, 0, 0), axis=along)]
    all_gather x1, waiting for transfers between devices: 66.6 us -> 0.02 us  [on_device(): lax.all_gather(adapter_up, 'group', axis=0, tiled=True)]
    all_gather x1 -> x0, waiting for transfers between devices: 60 us -> none  [on_device(): lax.all_gather(adapter_down, 'group', axis=0, tiled=True)]
    all_to_all x0 -> x1, starting transfers between devices: none -> 11.5 us  [swapped_in(): return jnp.concatenate(lax.all_to_all(repeated, axis, 0, 0), axis=along)]
    another operation x0 -> x1, local copies, waits for them, and re-layouts: none -> 4.33 us  [swapped_in(): repeated = jnp.stack([x] * lax.axis_size(axis))]
  transfers between devices with their start and end apart: 3 -> 3, of which waited for: 3 -> 2; matrix products, arithmetic and copies ran while one was open for 16% -> 18% of each run, Pallas kernels for 0% -> 0%
where the time goes in v1:
time: 289 us
  waiting for transfers between devices  137 us (47%)
  blocking collectives  64.5 us (22%)
  local copies, waits for them, and re-layouts  33.9 us (12%)
  matrix products  28.3 us (10%)
  between operations  13.5 us (5%)
  starting transfers between devices  11.6 us (4%)
    all_to_all x1, waiting for transfers between devices, swapped_in(): return jnp.concatenate(lax.all_to_all(repeated, axis, 0, 0), axis=along)  80.9 us
    psum x1, blocking collectives, on_device(): total_output = lax.psum(partial_value, 'tp')  64.5 us
    all_gather x1, waiting for transfers between devices, on_device(): lax.all_gather(tokens, 'tp', axis=1, tiled=True)  54.8 us
    gather x1, local copies, waits for them, and re-layouts, on_device(): picked_down = jnp.take(pool_down, adapter_id, axis=0)  22.5 us
    all_to_all x1, starting transfers between devices, swapped_in(): return jnp.concatenate(lax.all_to_all(repeated, axis, 0, 0), axis=along)  11.5 us
    dot_general x1, matrix products, on_device(): jnp.dot(lax.all_gather(tokens, 'tp', axis=1, tiled=True), w_query, prefer...  9.92 us
    dot_general x1, matrix products, on_device(): jnp.einsum('nd,nrd->nr', tokens, picked_down, preferred_element_type=jnp....  9.88 us
    dot_general x1, matrix products, on_device(): jnp.einsum('nr,nrh->nh', scaled_delta, picked_up, preferred_element_type=...  8.51 us
  transfers between devices with their start and end apart: 3, of which 2 were waited for; matrix products, arithmetic and copies ran while one was open for 18% of the time, Pallas kernels for 0%

profile of v1, /device:TPU:1, one launch (start us, length us, event | category | flops | bytes accessed | tf_op | source)
XLA Modules:
  0.0 288.9 jit_solution(17714049606796339259)
XLA Ops:
  6.5 0.0 all-gather.5.cloned.1.call-start
  6.5 0.7 all-gather.5.cloned.1.call-update
  7.3 0.0 all-gather.3.cloned.1.call-start
  7.3 0.7 all-gather.3.cloned.1.call-update
  8.0 4.3 %stack.2 = bf16[32,12,16,512]{3,2,1,0:T(8,128)(2,1)} broadcast(bf16[12,16,512]{2,1,0:T(8,128)(2,1)} %param.7), dimensions={1,2,3} | broadcast | bytes 6488064 | tf_op jit(solution)/shard_map/stack | solution.py:10
  12.3 0.0 copy-start.1
  12.3 11.5 %all-to-all-start = ((bf16[32,12,16,512]{3,2,1,0:T(8,128)(2,1)}), bf16[32,12,16,512]{3,2,1,0:T(8,128)(2,1)}, u32[]{:S(2)}, u32[]{:S(2)}) async-start(bf16[32,12,16,512]{3,2,1,0:T(8,128)(2,1)} %stack.2), calls=%async_computation | async-start | bytes 12582912 | tf_op jit(solution)/shard_map/all_to_all | solution.py:11
  23.9 0.0 copy-done.1
  23.9 80.9 %all-to-all-done = bf16[32,12,16,512]{3,2,1,0:T(8,128)(2,1)} async-done(((bf16[32,12,16,512]{3,2,1,0:T(8,128)(2,1)}), bf16[32,12,16,512]{3,2,1,0:T(8,128)(2,1)}, u32[]{:S(2)}, u32[]{:S(2)}) %all-to-all-start) | async-done | bytes 6291488 | tf_op jit(solution)/shard_map/all_to_all | solution.py:11
  104.8 22.5 %gather_fusion = bf16[768,16,512]{2,1,0:T(8,128)(2,1)} fusion(bf16[384,16,512]{2,1,0:T(8,128)(2,1)} %bitcast, s32[1024]{0:T(1024)S(1)} %pad_clamp_fusion), kind=kCustom, calls=%fused_computation | custom fusion | bytes 25168896 | tf_op jit(solution)/shard_map/jit(_take)/gather | solution.py:19
  127.4 0.0 copy-start
  127.4 0.0 all-gather.5.cloned.1.call-done
  127.4 7.0 %gather_fusion.1 = bf16[768,16,256]{2,1,0:T(8,128)(2,1)} fusion(bf16[384,16,256]{2,1,0:T(8,128)(2,1)} %all-gather.5.cloned.1.call-done, s32[1024]{0:T(1024)S(1)} %pad_clamp_fusion), kind=kCustom, calls=%fused_computation.1 | custom fusion | bytes 12585984 | tf_op jit(solution)/shard_map/jit(_take)/gather | solution.py:25
  134.4 0.0 copy-done
  134.4 9.9 %fusion = f32[768,1,16]{2,1,0:T(1,128)S(1)} fusion(bf16[768,16,512]{2,1,0:T(8,128)(2,1)} %gather_fusion, pred[768]{0:T(1024)(128)(4,1)S(1)} %compare_and_fusion, bf16[768,512,1]{1,0,2:T(8,128)(2,1)S(1)} %bitcast.12), kind=kOutput, calls=%fused_computation.2 | convolution fusion | flops 18874368 | bytes 13419264 | tf_op jit(solution)/shard_map/nd,nrd->nr/dot_general | solution.py:20
  144.3 64.5 %psum.7 = f32[768,16]{1,0:T(8,128)S(1)} all-reduce(f32[768,16]{1,0:T(8,128)S(1)} %bitcast.13), channel_id=1, replica_groups=mesh['group'=32,'tp'=16] {'tp'}, use_global_device_ids=true, to_apply=%region_0.1 | all-reduce | flops 12288 | bytes 98304 | tf_op jit(solution)/shard_map/psum | solution.py:23
  208.8 8.5 %fusion.3 = bf16[768,1,256]{2,1,0:T(2,128)(2,1)S(1)} fusion(bf16[768,16,256]{2,1,0:T(8,128)(2,1)} %gather_fusion.1, pred[768]{0:T(1024)(128)(4,1)S(1)} %compare_and_fusion, bf16[768,16,1]{1,0,2:T(8,128)(2,1)S(1)} %fusion.11), kind=kOutput, calls=%fused_computation.5 | convolution fusion | flops 9437184 | bytes 6710016 | tf_op jit(solution)/shard_map/nr,nrh->nh/dot_general | solution.py:26
  217.3 54.8 %all-gather.3.cloned.1.call-done = bf16[768,8192]{1,0:T(8,128)(2,1)} async-done(((bf16[768,512]{1,0:T(8,128)(2,1)}), bf16[768,8192]{1,0:T(8,128)(2,1)}) %all-gather.3.cloned.1.call-update) | async-done | bytes 12582928 | tf_op jit(solution)/shard_map/all_gather | solution.py:30
  272.2 9.9 %fusion.9 = bf16[768,256]{1,0:T(8,128)(2,1)} fusion(bf16[768,8192]{1,0:T(8,128)(2,1)} %all-gather.3.cloned.1.call-done, bf16[8192,256]{1,0:T(8,128)(2,1)} %param.6, bf16[768,1,256]{2,1,0:T(2,128)(2,1)S(1)} %fusion.3), kind=kOutput, calls=%fused_computation.12 | convolution fusion | flops 3221815296 | bytes 17563648 | tf_op jit(solution)/shard_map/dot_general | solution.py:29
  (4 shorter events, 0.0 us)
Async XLA Ops:
  6.5 120.9 %all-gather.5.cloned.1.call-start = ((), (), s32[]{:S(2)}) async-start(), calls=%async_computation.2 | async-start | bytes 3244032 | tf_op jit(solution)/shard_map/all_gather | solution.py:17
  7.3 264.9 %all-gather.3.cloned.1.call-start = ((), (), s32[]{:S(2)}) async-start(), calls=%async_computation.1 | async-start | bytes 13369344 | tf_op jit(solution)/shard_map/all_gather | solution.py:30
  12.3 11.5 %copy-start.1 = (s32[768]{0:T(1024)S(1)}, s32[768]{0:T(1024)}, u32[]{:S(2)}) copy-start(s32[768]{0:T(1024)} %param.9) | copy-start | bytes 9220
  12.3 92.5 %all-to-all-start = ((bf16[32,12,16,512]{3,2,1,0:T(8,128)(2,1)}), bf16[32,12,16,512]{3,2,1,0:T(8,128)(2,1)}, u32[]{:S(2)}, u32[]{:S(2)}) async-start(bf16[32,12,16,512]{3,2,1,0:T(8,128)(2,1)} %stack.2), calls=%async_computation | async-start | bytes 12582912 | tf_op jit(solution)/shard_map/all_to_all | solution.py:11
  127.4 7.1 %copy-start = (bf16[768,512]{1,0:T(8,128)(2,1)S(1)}, bf16[768,512]{1,0:T(8,128)(2,1)}, u32[]{:S(2)}) copy-start(bf16[768,512]{1,0:T(8,128)(2,1)} %param.5) | copy-start | bytes 2359300
Sparse Core Ops, SparseCore 0:
  10.5 103.2 all-gather.4
  115.9 156.2 all-gather.2
